TPU v7x, 32 devices: a whole 2x2x4 slice. The times are simulated.
32 devices in a mesh: seq: 4 (over x, core), head: 8 (over z, y).
Axes of the slice: x: 2, y: 2, z: 4, core: 2. Of those that a mesh axis runs over, the one named last changes fastest.
Arguments:
- features: bfloat16 [16384, 12288], P(('seq', 'head')), may hold values from -6 to 6
- selector: bfloat16 [16384, 256], P(('seq', 'head')), may hold values from -6 to 6
- step_input: bfloat16 [16384, 96], P(('seq', 'head')), may hold values from -2 to 20
- feature_kernel: float32 [4, 12288], replicated, may hold values from -3 to 3
- selector_kernel: float32 [4, 256], replicated, may hold values from -3 to 3
- feature_offset: float32 [12288], replicated, may hold values from -3 to 3
- selector_offset: float32 [256], replicated, may hold values from -3 to 3
- decay_log: float32 [96], replicated, may hold values from -2.4 to 0.1
- step_offset: float32 [96], replicated, may hold values from -12 to -2
- skip_scale: float32 [96], replicated, may hold values from 0.5 to 1.5
- norm_gain: float32 [12288], replicated, may hold values from 0.5 to 1.5
Outputs:
- output: bfloat16 [16384, 12288], P(('seq', 'head'))
All inputs are finite; a program needn't handle non-finite values.
Results may differ from a plain program's by a relative error of at most 0.008.
Values may be sent and summed in bfloat16 or wider, within the bound.
No kernel may reach another device: no remote copies, remote signals or barrier semaphores. Data moves between devices by JAX's collectives and lax.ppermute only.
A program may use at most 192 MiB of HBM per device.

v0:
```python
import math
import jax
import jax.numpy as jnp
from jax import lax
from jax.sharding import PartitionSpec as P

SPAN = 256


def passed_along(shard, axis, by):
    peers = lax.axis_size(axis)
    pairs = [(i, i + by) for i in range(peers) if 0 <= i + by < peers]
    return lax.ppermute(shard, axis, pairs)


def entering_2(shard, axis, join, neutral):
    place = lax.axis_index(axis)
    gathered = jax.tree.map(
        lambda a, kind: lax.all_gather(a.astype(kind), axis), shard, (jnp.bfloat16, jnp.bfloat16)
    )
    state = jax.tree.map(lambda a, e: jnp.zeros_like(a) + jnp.asarray(e, a.dtype), shard, neutral)

    def one(turn, state):
        return join(
            state,
            jax.tree.map(
                lambda a, own: lax.dynamic_index_in_dim(a, turn, 0, False).astype(own.dtype),
                gathered,
                shard,
            ),
        )

    return lax.fori_loop(0, place, one, state)


def causal_filter(tail_rows, new_rows, kernel, offset):
    length = new_rows.shape[0]
    window = jnp.concatenate([tail_rows, new_rows], axis=0).astype(jnp.float32)
    summed = jnp.broadcast_to(offset[None, :], (length, offset.shape[0]))
    for delay_step in range(kernel.shape[0]):
        summed = summed + kernel[delay_step][None, :] * window[delay_step : delay_step + length]
    return jax.nn.silu(summed).astype(jnp.bfloat16)


def normalize(values, norm_gain):
    widened = values.astype(jnp.float32)
    square = jnp.mean(widened * widened, axis=-1, keepdims=True)
    return (widened * lax.rsqrt(square + 1e-05) * norm_gain[None, :]).astype(jnp.bfloat16)


def join_states(former, latter):
    return (former[0] + latter[0], jnp.exp(latter[0])[:, None, None] * former[1] + latter[1])


def span_terms(feature_matrix_rows, write_rows, read_rows, step_size, log_decay):
    length = feature_matrix_rows.shape[0]
    head_count = step_size.shape[1]
    head_view = feature_matrix_rows.reshape(length, head_count, -1)
    cumulative = jnp.cumsum(log_decay, axis=0)
    inputs = (step_size[:, :, None] * head_view).astype(jnp.bfloat16)
    scores = jnp.dot(read_rows, write_rows.T, preferred_element_type=jnp.float32)
    log_spacing = cumulative.T[:, :, None] - cumulative.T[:, None, :]
    causal = jnp.arange(length)[:, None] >= jnp.arange(length)[None, :]
    decay_mask = jnp.exp(jnp.where(causal[None], log_spacing, -jnp.inf))
    mixing = (scores[None] * decay_mask).astype(jnp.bfloat16)
    diagonal = jnp.einsum("hij,jhp->ihp", mixing, inputs, preferred_element_type=jnp.float32)
    log_total = cumulative[-1]
    weighted = (
        (step_size * jnp.exp(log_total[None, :] - cumulative))[:, :, None] * head_view
    ).astype(jnp.bfloat16)
    span_state = jnp.einsum("jn,jhp->hnp", write_rows, weighted, preferred_element_type=jnp.float32)
    return (diagonal, cumulative, span_state, log_total)


def group_spans(values, span_count, group_size):
    return values.reshape((span_count // group_size, group_size, SPAN) + values.shape[1:])


def ungroup(values, span_count):
    return values.reshape((span_count,) + values.shape[2:])


def chain_states(span_states, log_totals):

    def advance(running, record):
        span_state, log_total = record
        return (jnp.exp(log_total)[:, None, None] * running + span_state, running)

    final_state, entering = lax.scan(
        advance, jnp.zeros_like(span_states[0]), (span_states, log_totals)
    )
    before = jnp.cumsum(log_totals, axis=0) - log_totals
    return (entering, before, final_state, jnp.sum(log_totals, axis=0))


def selective_rows(
    feature_conv, selector_conv, step_rows, decay_log, step_offset, skip_scale, carry_fn
):
    state_size = selector_conv.shape[1] // 2
    row_count = feature_conv.shape[0]
    span_count = row_count // SPAN
    group_size = math.gcd(span_count, 8)
    step_size = jax.nn.softplus(step_rows.astype(jnp.float32) + step_offset[None, :])
    log_decay = -jnp.exp(decay_log)[None, :] * step_size
    feature_groups = group_spans(feature_conv, span_count, group_size)
    read_groups = group_spans(selector_conv[:, state_size:], span_count, group_size)
    write_groups = group_spans(selector_conv[:, :state_size], span_count, group_size)

    def run_terms(group_items):
        return jax.vmap(span_terms)(*group_items)

    pieces = (
        feature_groups,
        write_groups,
        read_groups,
        group_spans(step_size, span_count, group_size),
        group_spans(log_decay, span_count, group_size),
    )
    diagonal, cumulative, span_states, log_totals = lax.map(run_terms, pieces)
    span_states = ungroup(span_states, span_count)
    log_totals = ungroup(log_totals, span_count)
    entering, before, final_state, block_log = chain_states(span_states, log_totals)
    state_in = carry_fn(block_log, final_state)

    def one_span(diag_rows, cumul_rows, read_rows, state_local, log_before, feature_matrix_rows):
        length, head_count, head_width = diag_rows.shape
        entry_state = state_local + jnp.exp(log_before)[:, None, None] * state_in
        carried = jnp.einsum(
            "in,hnp->ihp",
            read_rows,
            entry_state.astype(jnp.bfloat16),
            preferred_element_type=jnp.float32,
        )
        head_view = feature_matrix_rows.reshape(length, head_count, head_width).astype(jnp.float32)
        summed = (
            diag_rows
            + jnp.exp(cumul_rows)[:, :, None] * carried
            + skip_scale[None, :, None] * head_view
        )
        return summed.reshape(length, head_count * head_width).astype(jnp.bfloat16)

    def run_output(group_items):
        return jax.vmap(one_span)(*group_items)

    regroup_entering = entering.reshape((span_count // group_size, group_size) + entering.shape[1:])
    regroup_before = before.reshape((span_count // group_size, group_size) + before.shape[1:])
    results = lax.map(
        run_output,
        (diagonal, cumulative, read_groups, regroup_entering, regroup_before, feature_groups),
    )
    return results.reshape(row_count, -1)


def token_conv(
    features, selector, feature_kernel, selector_kernel, feature_offset, selector_offset
):
    tail_count = feature_kernel.shape[0] - 1
    channels = features.shape[1]
    row_count = features.shape[0]
    last_rows = jnp.concatenate(
        [features[row_count - tail_count :], selector[row_count - tail_count :]], axis=1
    )
    tail_rows = passed_along(last_rows, ("seq", "head"), 1)
    feature_conv = causal_filter(tail_rows[:, :channels], features, feature_kernel, feature_offset)
    selector_conv = causal_filter(
        tail_rows[:, channels:], selector, selector_kernel, selector_offset
    )
    return (feature_conv, selector_conv)


def on_device(
    features,
    selector,
    step_input,
    feature_kernel,
    selector_kernel,
    feature_offset,
    selector_offset,
    decay_log,
    step_offset,
    skip_scale,
    norm_gain,
):
    head_count = decay_log.shape[0] // lax.axis_size("head")
    head_first = lax.axis_index("head") * head_count
    feature_send, selector_send = token_conv(
        features, selector, feature_kernel, selector_kernel, feature_offset, selector_offset
    )
    feature_slab, step_slab = (
        lax.all_to_all(feature_send, "head", split_axis=1, concat_axis=0, tiled=True),
        lax.all_to_all(step_input, "head", split_axis=1, concat_axis=0, tiled=True),
    )
    selector_slab = lax.all_gather(selector_send, "head", axis=0, tiled=True)
    feature_conv, selector_conv = (feature_slab, selector_slab)
    own_decay = lax.dynamic_slice_in_dim(decay_log, head_first, head_count, axis=0)
    own_step = lax.dynamic_slice_in_dim(step_offset, head_first, head_count, axis=0)
    own_skip = lax.dynamic_slice_in_dim(skip_scale, head_first, head_count, axis=0)

    def slab_prefix(block_log, final_state):
        prefix = entering_2(
            (block_log, final_state),
            "seq",
            join_states,
            (jnp.zeros_like(block_log), jnp.zeros_like(final_state)),
        )
        return prefix[1]

    mixed = selective_rows(
        feature_conv, selector_conv, step_slab, own_decay, own_step, own_skip, slab_prefix
    )
    blended_rows = lax.all_to_all(mixed, "head", split_axis=0, concat_axis=1, tiled=True)
    return normalize(blended_rows, norm_gain)


def solution(mesh):
    placed = (
        P(("seq", "head"), None),
        P(("seq", "head"), None),
        P(("seq", "head"), None),
        P(),
        P(),
        P(),
        P(),
        P(),
        P(),
        P(),
        P(),
    )
    return jax.shard_map(
        on_device, mesh=mesh, in_specs=placed, out_specs=P(("seq", "head"), None), check_vma=False
    )
```

profile of v0, /device:TPU:7, one launch (start us, length us, event | category | flops | bytes accessed | tf_op | source)
XLA Modules:
  0.0 1045.2 jit_solution(126070698641346954)
XLA Ops:
  20.9 16.6 %copy.85 = bf16[512,12288]{0,1:T(8,128)(2,1)} copy(bf16[512,12288]{1,0:T(8,128)(2,1)} %param.19) | data formatting | bytes 25165824 | tf_op args[0]
  39.8 17.2 %maximum_convert_fusion = f32[515,12288]{0,1:T(8,128)} fusion(bf16[512,12288]{0,1:T(8,128)(2,1)} %copy.85, bf16[3,12288]{0,1:T(8,128)(2,1)S(1)} %copy.84), kind=kLoop, calls=%fused_computation.78 | loop fusion | flops 25313280 | bytes 37969920 | tf_op jit(solution)/shard_map/convert_element_type | solution.py:38
  57.0 59.4 %multiply_convert_fusion.4 = bf16[512,12288]{0,1:T(8,128)(2,1)} fusion(f32[515,12288]{0,1:T(8,128)} %maximum_convert_fusion, f32[12288]{0:T(1024)S(1)} %bitcast.193, f32[12288]{0:T(1024)S(1)} %bitcast.194, f32[12288]{0:T(1024)S(1)} %bitcast.192, f32[12288]{0:T(1024)S(1)} %bitcast.191, f32[12288]{0:T(1024)S(1)} %copy-done.10), kind=kLoop, calls=%fused_computation.77 | loop fusion | flops 81788928 | bytes 113491968 | tf_op jit(solution)/shard_map/convert_element_type | solution.py:42
  124.9 238.1 %all-gather.5.cloned.1.call-done = bf16[4096,256]{1,0:T(8,128)(2,1)} async-done(((bf16[512,256]{1,0:T(8,128)(2,1)}), bf16[4096,256]{1,0:T(8,128)(2,1)}) %all-gather.5.cloned.1.call-update) | async-done | bytes 2097168 | tf_op jit(solution)/shard_map/all_gather | solution.py:193
  364.7 55.1 %all-to-all-done.1 = bf16[512,8,1536]{0,2,1:T(8,128)(2,1)} async-done(((bf16[512,8,1536]{0,2,1:T(8,128)(2,1)}), bf16[512,8,1536]{0,2,1:T(8,128)(2,1)}, u32[]{:S(2)}, u32[]{:S(2)}) %all-to-all-start.1) | async-done | bytes 12582944 | tf_op jit(solution)/shard_map/all_to_all | solution.py:190
  419.9 16.7 %copy.86 = bf16[8,512,1536]{2,1,0:T(8,128)(2,1)} copy(bf16[8,512,1536]{1,2,0:T(8,128)(2,1)} %bitcast.40) | data formatting | bytes 25165824 | tf_op jit(solution)/shard_map/all_to_all | solution.py:190
  436.5 15.7 %copy.89 = bf16[2,8,256,1536]{2,3,1,0:T(8,128)(2,1)} copy(bf16[2,8,256,1536]{3,2,1,0:T(8,128)(2,1)} %bitcast.181) | data formatting | bytes 25165824 | tf_op jit(solution)/shard_map/while | solution.py:119
  452.2 76.1 %while.51 = (s32[]{:T(128)}, f32[2,8,256,12,128]{2,4,3,1,0:T(8,128)}, f32[2,8,256,12]{2,1,3,0:T(8,128)}, f32[2,8,12,128,128]{4,3,2,1,0:T(8,128)}, f32[2,8,12]{2,...) while((s32[]{:T(128)}, ...), condition=%wide.region_3.4_spmd, body=%wide.region_0.3_spmd.sunk | while | flops 2597437696 | bytes 77813640 | solution.py:119
  462.4 9.7 bitcast_dynamic-update-slice_fusion.8
  476.6 6.5 copy.142
  483.1 6.3 constant_dynamic-update-slice_fusion.4
  500.4 9.7 bitcast_dynamic-update-slice_fusion.8
  514.6 6.5 copy.142
  521.1 6.3 constant_dynamic-update-slice_fusion.4
  528.3 36.3 %while.54 = (s32[]{:T(128)}, f32[12,128,128]{2,1,0:T(8,128)S(1)}, f32[16,12,128,128]{3,2,1,0:T(8,128)}, f32[16,12]{1,0:T(8,128)S(1)}, f32[16,12,128,128]{3,2,1,0:T(8,128)}, /*index=5*/s32[]{:T(128)}, s32[]{:T(128)}) while((s32[]{:T(128)}, f32[12,128,128]{2,1,0:T(8,128)S(1)}, f32[16,12,128,128]{3,2,1,0:T(8,128)}, ...), condition=%wide.region_5.6_spmd.clone, body=%wide.region_4.5_spmd.clone.sunk | while | flops 786435 | bytes 3932912 | solution.py:89
  567.0 6.4 all-reduce
  573.5 10.8 %all-gather.7.cloned.1.call-done = bf16[48,128,128]{2,1,0:T(8,128)(2,1)} async-done(((bf16[12,128,128]{2,1,0:T(8,128)(2,1)}), bf16[48,128,128]{2,1,0:T(8,128)(2,1)}) %all-gather.7.cloned.1.call-update) | async-done | bytes 1572880 | tf_op jit(solution)/shard_map/all_gather | solution.py:19
  588.7 94.6 %while.53 = (s32[]{:T(128)}, bf16[2,8,256,1536]{3,2,1,0:T(8,128)(2,1)}, f32[2,8,256,12,128]{2,4,3,1,0:T(8,128)}, f32[2,8,256,12]{2,1,3,0:T(8,128)S(1)}, bf16[2,8...) while((s32[]{:T(128)}, ...), condition=%wide.region_11.12_spmd, body=%wide.region_10.11_spmd.sunk | while | flops 828899328 | bytes 142313392 | solution.py:147
  588.7 6.9 constant_dynamic-slice_fusion.11
  595.6 6.5 copy.145
  610.8 10.5 %fusion.86 = bf16[8,256,12,128]{1,3,2,0:T(8,128)(2,1)} fusion(bf16[8,256,12,128]{1,3,2,0:T(8,128)(2,1)S(1)} %bitcast.176, f32[8,256,12,128]{1,3,2,0:T(8,128)S(1)} %bitcast.173, f32[2,8,256,12,128]{2,4,3,1,0:T(8,128)} %get-tuple-element.654, s32[]{:T(128)} %get-tuple-element.641, f32[12]{0:T(128)S(1)} %get-tuple-element.660, f32[8,256,12]{1,2,0:T(8,128)S(1)} %fusion.85), kind=kLoop, calls=%fused_computation.43.clone.1 | loop fusion | flops 18874368 | bytes 37847092 | tf_op jit(solution)/shard_map/while/body/eval_jaxpr/vmap()/convert_element_type | solution.py:140
  621.3 8.8 copy.146
  636.0 6.9 constant_dynamic-slice_fusion.11
  642.9 6.5 copy.145
  658.1 10.5 %fusion.86 = bf16[8,256,12,128]{1,3,2,0:T(8,128)(2,1)} fusion(bf16[8,256,12,128]{1,3,2,0:T(8,128)(2,1)S(1)} %bitcast.176, f32[8,256,12,128]{1,3,2,0:T(8,128)S(1)} %bitcast.173, f32[2,8,256,12,128]{2,4,3,1,0:T(8,128)} %get-tuple-element.654, s32[]{:T(128)} %get-tuple-element.641, f32[12]{0:T(128)S(1)} %get-tuple-element.660, f32[8,256,12]{1,2,0:T(8,128)S(1)} %fusion.85), kind=kLoop, calls=%fused_computation.43.clone.1 | loop fusion | flops 18874368 | bytes 37847092 | tf_op jit(solution)/shard_map/while/body/eval_jaxpr/vmap()/convert_element_type | solution.py:140
  668.6 8.8 copy.146
  683.2 278.8 %all_to_all.42 = bf16[8,512,1536]{2,1,0:T(8,128)(2,1)S(1)} all-to-all(bf16[8,512,1536]{2,1,0:T(8,128)(2,1)} %bitcast.187), channel_id=1, replica_groups=mesh['seq'=4,'head'=8] {'head'}, dimensions={0} | all-to-all | bytes 25165824 | tf_op jit(solution)/shard_map/all_to_all | solution.py:211
  966.8 9.4 convert_bitcast_fusion
  976.2 24.7 %copy.97 = f32[512,8,1536]{0,2,1:T(8,128)} copy(f32[512,8,1536]{2,0,1:T(8,128)} %convert_bitcast_fusion) | data formatting | bytes 50331648 | tf_op jit(solution)/shard_map/convert_element_type | solution.py:46
  1000.9 7.1 fusion.40
  1008.1 13.7 %fusion.46 = bf16[512,12288]{0,1:T(8,128)(2,1)} fusion(f32[512,8,1536]{0,2,1:T(8,128)} %copy.97, f32[12288]{0:T(1024)S(1)} %copy-done.11, f32[512]{0:T(512)S(1)} %add_rsqrt_fusion), kind=kLoop, calls=%fused_computation.76 | loop fusion | flops 18874368 | bytes 37799936 | tf_op jit(solution)/shard_map/convert_element_type | solution.py:48
  1021.8 16.6 %copy.98 = bf16[512,12288]{1,0:T(8,128)(2,1)} copy(bf16[512,12288]{0,1:T(8,128)(2,1)} %fusion.46) | data formatting | bytes 25165824 | tf_op jit(solution)/shard_map/convert_element_type | solution.py:48
  (205 shorter events, 137.1 us)
Async XLA Ops:
  8.1 108.3 %all-to-all-start = ((bf16[512,8,12]{0,2,1:T(8,128)(2,1)}), bf16[512,8,12]{0,2,1:T(8,128)(2,1)S(1)}, u32[]{:S(2)}, u32[]{:S(2)}) async-start(bf16[512,8,12]{0,2,1:T(8,128)(2,1)} %all_to_all.32), calls=%async_computation | async-start | bytes 262144 | tf_op jit(solution)/shard_map/all_to_all | solution.py:191
  15.6 21.9 %collective-permute-start = (bf16[3,12544]{1,0:T(4,128)(2,1)S(1)}, bf16[3,12544]{1,0:T(4,128)(2,1)S(1)}, u32[]{:S(2)}, u32[]{:S(2)}) collective-permute-start(bf16[3,12544]{1,0:T(4,128)(2,1)S(1)} %pad_maximum_fusion), channel_id=1, source_target_pairs={{0,1},{1,2},{2,3},{3,4},{4,5},{5,6},{6,7},{7,8},{8,9},{9,10},{10,1... | collective-permute-start | bytes 225800 | tf_op jit(solution)/shard_map/ppermute | solution.py:13
  37.5 0.6 copy-start.9
  39.8 17.2 %copy-start.8 = (f32[1,12288]{1,0:T(1,128)S(1)}, f32[1,12288]{1,0:T(1,128)}, u32[]{:S(2)}) copy-start(f32[1,12288]{1,0:T(1,128)} %get-tuple-element.351) | copy-start | bytes 147460
  39.8 17.2 %copy-start.10 = (f32[12288]{0:T(1024)S(1)}, f32[12288]{0:T(1024)}, u32[]{:S(2)}) copy-start(f32[12288]{0:T(1024)} %param.24) | copy-start | bytes 147460
  116.4 5.8 copy-start.12
  116.4 5.8 copy-start.7
  116.5 5.8 slice-start
  116.5 5.8 copy-start.13
  116.5 7.2 copy-start.14
  116.5 7.3 copy-start.15
  116.5 303.4 %all-to-all-start.1 = ((bf16[512,8,1536]{0,2,1:T(8,128)(2,1)}), bf16[512,8,1536]{0,2,1:T(8,128)(2,1)}, u32[]{:S(2)}, u32[]{:S(2)}) async-start(bf16[512,8,1536]{0,2,1:T(8,128)(2,1)} %bitcast.180), calls=%async_computation.1 | async-start | bytes 25165824 | tf_op jit(solution)/shard_map/all_to_all | solution.py:190
  122.2 240.9 %all-gather.5.cloned.1.call-start = ((), (), s32[]{:S(2)}) async-start(), calls=%async_computation.3 | async-start | bytes 2359296 | tf_op jit(solution)/shard_map/all_gather | solution.py:193
  123.4 461.0 %all-gather.7.cloned.1.call-start = ((), (), s32[]{:S(2)}) async-start(), calls=%async_computation.4 | async-start | bytes 1966080 | tf_op jit(solution)/shard_map/all_gather | solution.py:19
  452.2 76.1 %copy-start.1 = (f32[12,128,128]{2,1,0:T(8,128)S(1)}, f32[12,128,128]{2,1,0:T(8,128)}, u32[]{:S(2)}) copy-start(f32[12,128,128]{2,1,0:T(8,128)} %custom-call) | copy-start | bytes 2359300
  528.3 37.2 %copy-start.16 = (f32[96]{0:T(128)S(1)}, f32[96]{0:T(128)}, u32[]{:S(2)}) copy-start(f32[96]{0:T(128)} %param.28) | copy-start | bytes 1156
  528.3 37.2 %copy-start.17 = (u32[32]{0:T(128)S(1)}, u32[32]{0:T(128)}, u32[]{:S(2)}) copy-start(u32[32]{0:T(128)} %constant.111) | copy-start | bytes 388
  528.3 60.4 %copy-start.6 = (f32[2,8,256,12]{2,1,3,0:T(8,128)S(1)}, f32[2,8,256,12]{2,1,3,0:T(8,128)}, u32[]{:S(2)}) copy-start(f32[2,8,256,12]{2,1,3,0:T(8,128)} %get-tuple-element.633) | copy-start | bytes 589828
  588.7 13.4 %copy-start.4 = (f32[12,128,128]{1,2,0:T(8,128)}, f32[12,128,128]{1,2,0:T(8,128)S(1)}, u32[]{:S(2)}) copy-start(f32[12,128,128]{1,2,0:T(8,128)S(1)} %get-tuple-element.659) | copy-start | bytes 2359300 | tf_op jit(solution)/shard_map/while
  588.7 17.0 %copy-start.2 = (bf16[2,8,256,128]{3,2,1,0:T(8,128)(2,1)}, bf16[2,8,256,128]{3,2,1,0:T(8,128)(2,1)S(1)}, u32[]{:S(2)}) copy-start(bf16[2,8,256,128]{3,2,1,0:T(8,128)(2,1)S(1)} %get-tuple-element.656) | copy-start | bytes 3145732 | tf_op jit(solution)/shard_map/while
  621.3 14.7 %copy-start.3 = (bf16[2,8,256,128]{3,2,1,0:T(8,128)(2,1)S(1)}, bf16[2,8,256,128]{3,2,1,0:T(8,128)(2,1)}, u32[]{:S(2)}) copy-start(bf16[2,8,256,128]{3,2,1,0:T(8,128)(2,1)} %copy-done.2) | copy-start | bytes 3145732 | tf_op jit(solution)/shard_map/while
  621.3 14.7 %copy-start.5 = (f32[12,128,128]{1,2,0:T(8,128)S(1)}, f32[12,128,128]{1,2,0:T(8,128)}, u32[]{:S(2)}) copy-start(f32[12,128,128]{1,2,0:T(8,128)} %copy-done.4) | copy-start | bytes 2359300 | tf_op jit(solution)/shard_map/while
  636.0 13.4 %copy-start.4 = (f32[12,128,128]{1,2,0:T(8,128)}, f32[12,128,128]{1,2,0:T(8,128)S(1)}, u32[]{:S(2)}) copy-start(f32[12,128,128]{1,2,0:T(8,128)S(1)} %get-tuple-element.659) | copy-start | bytes 2359300 | tf_op jit(solution)/shard_map/while
  636.0 17.0 %copy-start.2 = (bf16[2,8,256,128]{3,2,1,0:T(8,128)(2,1)}, bf16[2,8,256,128]{3,2,1,0:T(8,128)(2,1)S(1)}, u32[]{:S(2)}) copy-start(bf16[2,8,256,128]{3,2,1,0:T(8,128)(2,1)S(1)} %get-tuple-element.656) | copy-start | bytes 3145732 | tf_op jit(solution)/shard_map/while
  668.5 14.7 %copy-start.3 = (bf16[2,8,256,128]{3,2,1,0:T(8,128)(2,1)S(1)}, bf16[2,8,256,128]{3,2,1,0:T(8,128)(2,1)}, u32[]{:S(2)}) copy-start(bf16[2,8,256,128]{3,2,1,0:T(8,128)(2,1)} %copy-done.2) | copy-start | bytes 3145732 | tf_op jit(solution)/shard_map/while
  668.6 14.7 %copy-start.5 = (f32[12,128,128]{1,2,0:T(8,128)S(1)}, f32[12,128,128]{1,2,0:T(8,128)}, u32[]{:S(2)}) copy-start(f32[12,128,128]{1,2,0:T(8,128)} %copy-done.4) | copy-start | bytes 2359300 | tf_op jit(solution)/shard_map/while
  962.0 4.8 copy-start
  1000.9 7.1 copy-start.11
Sparse Core Ops, SparseCore 0:
  125.1 237.8 all-gather.4
  565.5 18.8 all-gather.6
where the time goes:
time: 1050 us
  waiting for transfers between devices  304 us (29%)
  blocking collectives  285 us (27%)
  local copies, waits for them, and re-layouts  204 us (19%)
  other arithmetic  189 us (18%)
  matrix products  32.8 us (3%)
  starting transfers between devices  14.8 us (1%)
  between operations  14.4 us (1%)
    all_to_all x1, blocking collectives, on_device(): lax.all_to_all(mixed, 'head', split_axis=0, concat_axis=1, tiled=True)  279 us
    all_gather x1, waiting for transfers between devices, on_device(): selector_slab = lax.all_gather(selector_send, 'head', axis=0, tiled=True)  238 us
    convert_element_type x2, other arithmetic, causal_filter(): return jax.nn.silu(summed).astype(jnp.bfloat16)  60.5 us
    all_to_all x1, waiting for transfers between devices, on_device(): lax.all_to_all(feature_send, 'head', split_axis=1, concat_axis=0, tiled=T...  55.1 us
    dynamic_update_slice x4, local copies, waits for them, and re-layouts, selective_rows(): lax.map(run_output, (diagonal, cumulative, read_groups, regroup_entering,...  29.4 us
    dynamic_update_slice x8, local copies, waits for them, and re-layouts, selective_rows(): diagonal, cumulative, span_states, log_totals = lax.map(run_terms, pieces)  27 us
    dynamic_slice x4, local copies, waits for them, and re-layouts, selective_rows(): lax.map(run_output, (diagonal, cumulative, read_groups, regroup_entering,...  26.8 us
    convert_element_type x1, local copies, waits for them, and re-layouts, normalize(): widened = values.astype(jnp.float32)  24.7 us
  transfers between devices with their start and end apart: 5, of which 3 were waited for; matrix products, arithmetic and copies ran while one was open for 10% of the time, Pallas kernels for 0%

commit v1 on v0

--- a/solution.py
+++ b/solution.py
@@ -1,3 +1,4 @@
+import functools
 import math
 import jax
 import jax.numpy as jnp
@@ -5,6 +6,35 @@
 from jax.sharding import PartitionSpec as P
 
 SPAN = 256
+
+
+def cards_pass(inp, dim_at, z_in):
+    val, current_arr = (inp.shape[:dim_at], inp.shape[dim_at + 1 :])
+    return jnp.moveaxis(inp.reshape(*val, z_in, -1, *current_arr), dim_at, 0)
+
+
+def post_vector(u, along_dim):
+    last = list(u.shape[1:])
+    last[along_dim] *= u.shape[0]
+    return jnp.moveaxis(u, 0, along_dim).reshape(last)
+
+
+def watch_packet(field_in, chip_axis, frame, xin):
+    reply, block_out = (lax.psum(1, chip_axis), lax.axis_index(chip_axis))
+    row_out = cards_pass(field_in, frame, reply)
+    block_list = [row_out[block_out]]
+    dev_i = 1
+    while dev_i < reply:
+        ready = row_out[block_out ^ dev_i]
+        block_list.append(
+            lax.ppermute(ready, chip_axis, perm=[(src_i, src_i ^ dev_i) for src_i in range(reply)])
+        )
+        dev_i += 1
+    row_out = jnp.stack(block_list)[block_out ^ jnp.arange(reply)]
+    return post_vector(row_out, xin)
+
+
+close_hubs = functools.partial(watch_packet, chip_axis="head", frame=1, xin=0)
 
 
 def passed_along(shard, axis, by):
@@ -187,7 +217,7 @@
         features, selector, feature_kernel, selector_kernel, feature_offset, selector_offset
     )
     feature_slab, step_slab = (
-        lax.all_to_all(feature_send, "head", split_axis=1, concat_axis=0, tiled=True),
+        close_hubs(feature_send),
         lax.all_to_all(step_input, "head", split_axis=1, concat_axis=0, tiled=True),
     )
     selector_slab = lax.all_gather(selector_send, "head", axis=0, tiled=True)

time: 1050 us -> 1060 us (level)
  waiting for transfers between devices: 304 us -> 267 us
  local copies, waits for them, and re-layouts: 204 us -> 238 us
  blocking collectives: 285 us -> 296 us
    all_gather x1, waiting for transfers between devices: 238 us -> 0.01 us  [on_device(): selector_slab = lax.all_gather(selector_send, 'head', axis=0, tiled=True)]
    ppermute x0 -> x7, waiting for transfers between devices: none -> 184 us  [watch_packet(): lax.ppermute(ready, chip_axis, perm=[(src_i, src_i ^ dev_i) for src_i in...]
    all_gather x1, waiting for transfers between devices: 10.8 us -> 83.2 us  [entering_2(): lax.all_gather(a.astype(kind), axis)]
    all_to_all x1 -> x0, waiting for transfers between devices: 55.1 us -> none  [on_device(): lax.all_to_all(feature_send, 'head', split_axis=1, concat_axis=0, tiled=T...]
    another operation x9 -> x19, local copies, waits for them, and re-layouts: 0.27 us -> 22.4 us
    all_to_all x1 -> x0, local copies, waits for them, and re-layouts: 16.7 us -> none  [on_device(): lax.all_to_all(feature_send, 'head', split_axis=1, concat_axis=0, tiled=T...]
    unnamed x32 -> x39, local copies, waits for them, and re-layouts: 22.9 us -> 39 us
    gather x0 -> x1, local copies, waits for them, and re-layouts: none -> 11 us  [watch_packet(): row_out = jnp.stack(block_list)[block_out ^ jnp.arange(reply)]]
  transfers between devices with their start and end apart: 5 -> 11, of which waited for: 3 -> 5; matrix products, arithmetic and copies ran while one was open for 10% -> 16% of each run, Pallas kernels for 0% -> 0%
where the time goes in v1:
time: 1060 us
  blocking collectives  296 us (28%)
  waiting for transfers between devices  267 us (25%)
  local copies, waits for them, and re-layouts  238 us (22%)
  other arithmetic  191 us (18%)
  matrix products  32.6 us (3%)
  starting transfers between devices  18.9 us (2%)
  between operations  14.3 us (1%)
    all_to_all x1, blocking collectives, on_device(): lax.all_to_all(mixed, 'head', split_axis=0, concat_axis=1, tiled=True)  279 us
    ppermute x7, waiting for transfers between devices, watch_packet(): lax.ppermute(ready, chip_axis, perm=[(src_i, src_i ^ dev_i) for src_i in...  184 us
    all_gather x1, waiting for transfers between devices, entering_2(): lax.all_gather(a.astype(kind), axis)  83.2 us
    convert_element_type x2, other arithmetic, causal_filter(): return jax.nn.silu(summed).astype(jnp.bfloat16)  61.7 us
    unnamed x39, local copies, waits for them, and re-layouts  39 us
    dynamic_update_slice x4, local copies, waits for them, and re-layouts, selective_rows(): lax.map(run_output, (diagonal, cumulative, read_groups, regroup_entering,...  29.5 us
    dynamic_update_slice x8, local copies, waits for them, and re-layouts, selective_rows(): diagonal, cumulative, span_states, log_totals = lax.map(run_terms, pieces)  27.2 us
    dynamic_slice x4, local copies, waits for them, and re-layouts, selective_rows(): lax.map(run_output, (diagonal, cumulative, read_groups, regroup_entering,...  26.9 us
  transfers between devices with their start and end apart: 11, of which 5 were waited for; matrix products, arithmetic and copies ran while one was open for 16% of the time, Pallas kernels for 0%

profile of v1, /device:TPU:7, one launch (start us, length us, event | category | flops | bytes accessed | tf_op | source)
XLA Modules:
  0.0 1058.3 jit_solution(2946174282600384753)
XLA Ops:
  17.8 16.7 %copy.92 = bf16[512,12288]{0,1:T(8,128)(2,1)} copy(bf16[512,12288]{1,0:T(8,128)(2,1)} %param.19) | data formatting | bytes 25165824 | tf_op args[0]
  38.9 17.2 %maximum_convert_fusion = f32[515,12288]{0,1:T(8,128)} fusion(bf16[512,12288]{0,1:T(8,128)(2,1)} %copy.92, bf16[3,12288]{0,1:T(8,128)(2,1)S(1)} %copy.91), kind=kLoop, calls=%fused_computation.79 | loop fusion | flops 25313280 | bytes 37969920 | tf_op jit(solution)/shard_map/convert_element_type | solution.py:68
  56.2 60.0 %multiply_convert_fusion.4 = bf16[512,12288]{0,1:T(8,128)(2,1)S(1)} fusion(f32[515,12288]{0,1:T(8,128)} %maximum_convert_fusion, f32[12288]{0:T(1024)S(1)} %bitcast.221, f32[12288]{0:T(1024)S(1)} %bitcast.222, f32[12288]{0:T(1024)S(1)} %bitcast.220, f32[12288]{0:T(1024)S(1)} %bitcast.219, f32[12288]{0:T(1024)S(1)} %copy-done.11), kind=kLoop, calls=%fused_computation.78 | loop fusion | flops 81788928 | bytes 113491968 | tf_op jit(solution)/shard_map/convert_element_type | solution.py:72
  147.7 8.6 collective-permute-done.1
  161.9 67.3 %collective-permute-done.2 = bf16[512,1536]{1,0:T(8,128)(2,1)} collective-permute-done((bf16[512,1536]{1,0:T(8,128)(2,1)}, bf16[512,1536]{1,0:T(8,128)(2,1)}, u32[]{:S(2)}, u32[]{:S(2)}) %collective-permute-start.2) | collective-permute-done | bytes 1572896 | tf_op jit(solution)/shard_map/ppermute | solution.py:30
  234.7 30.0 %collective-permute-done.3 = bf16[512,1536]{1,0:T(8,128)(2,1)} collective-permute-done((bf16[512,1536]{1,0:T(8,128)(2,1)}, bf16[512,1536]{1,0:T(8,128)(2,1)}, u32[]{:S(2)}, u32[]{:S(2)}) %collective-permute-start.3) | collective-permute-done | bytes 1572896 | tf_op jit(solution)/shard_map/ppermute | solution.py:30
  270.1 77.6 %collective-permute-done.5 = bf16[512,1536]{1,0:T(8,128)(2,1)} collective-permute-done((bf16[512,1536]{1,0:T(8,128)(2,1)}, bf16[512,1536]{1,0:T(8,128)(2,1)}, u32[]{:S(2)}, u32[]{:S(2)}) %collective-permute-start.5) | collective-permute-done | bytes 1572896 | tf_op jit(solution)/shard_map/ppermute | solution.py:30
  353.0 11.0 %gather_fusion = bf16[8,512,1536]{2,1,0:T(8,128)(2,1)} fusion(bf16[8,512,1536]{2,1,0:T(8,128)(2,1)} %bitcast_dynamic-update-slice_fusion.4, s32[1024]{0:T(1024)S(1)} %pad_clamp_fusion), kind=kCustom, calls=%fused_computation | custom fusion | bytes 25165856 | tf_op jit(solution)/shard_map/gather | solution.py:33
  364.0 16.6 %copy.103 = bf16[2,8,256,1536]{2,3,1,0:T(8,128)(2,1)} copy(bf16[2,8,256,1536]{3,2,1,0:T(8,128)(2,1)} %bitcast.205) | data formatting | bytes 25165824 | tf_op jit(solution)/shard_map/while | solution.py:149
  382.4 76.0 %while.51 = (s32[]{:T(128)}, f32[2,8,256,12,128]{2,4,3,1,0:T(8,128)}, f32[2,8,256,12]{2,1,3,0:T(8,128)}, f32[2,8,12,128,128]{4,3,2,1,0:T(8,128)}, f32[2,8,12]{2,...) while((s32[]{:T(128)}, ...), condition=%wide.region_3.4_spmd, body=%wide.region_0.3_spmd.sunk | while | flops 2597437696 | bytes 77813640 | solution.py:149
  392.6 9.7 bitcast_dynamic-update-slice_fusion.16
  406.7 6.6 copy.156
  430.6 9.6 bitcast_dynamic-update-slice_fusion.16
  444.7 6.6 copy.156
  458.4 36.3 %while.54 = (s32[]{:T(128)}, f32[12,128,128]{2,1,0:T(8,128)S(1)}, f32[16,12,128,128]{3,2,1,0:T(8,128)}, f32[16,12]{1,0:T(8,128)S(1)}, f32[16,12,128,128]{3,2,1,0:T(8,128)}, /*index=5*/s32[]{:T(128)}, s32[]{:T(128)}) while((s32[]{:T(128)}, f32[12,128,128]{2,1,0:T(8,128)S(1)}, f32[16,12,128,128]{3,2,1,0:T(8,128)}, ...), condition=%wide.region_5.6_spmd.clone, body=%wide.region_4.5_spmd.clone.sunk | while | flops 786435 | bytes 3932912 | solution.py:119
  497.3 16.9 %all-reduce = bf16[48]{0:T(256)(128)(2,1)S(1)} all-reduce(bf16[48]{0:T(256)(128)(2,1)S(1)} %dynamic-update-slice), channel_id=2, replica_groups=mesh['seq'=4,'head'=8] {'seq'}, use_global_device_ids=true, to_apply=%add | all-reduce | flops 48 | bytes 192
  514.3 83.2 %all-gather.7.cloned.1.call-done = bf16[48,128,128]{2,1,0:T(8,128)(2,1)} async-done(((bf16[12,128,128]{2,1,0:T(8,128)(2,1)}), bf16[48,128,128]{2,1,0:T(8,128)(2,1)}) %all-gather.7.cloned.1.call-update) | async-done | bytes 1572880 | tf_op jit(solution)/shard_map/all_gather | solution.py:49
  601.8 94.6 %while.53 = (s32[]{:T(128)}, bf16[2,8,256,1536]{3,2,1,0:T(8,128)(2,1)}, f32[2,8,256,12,128]{2,4,3,1,0:T(8,128)}, f32[2,8,256,12]{2,1,3,0:T(8,128)S(1)}, bf16[2,8...) while((s32[]{:T(128)}, ...), condition=%wide.region_11.12_spmd, body=%wide.region_10.11_spmd.sunk | while | flops 828899328 | bytes 142313392 | solution.py:177
  601.8 6.8 constant_dynamic-slice_fusion.19
  608.6 6.6 copy.159
  623.9 10.4 fusion.87
  634.3 8.8 copy.160
  649.1 6.8 constant_dynamic-slice_fusion.19
  655.9 6.6 copy.159
  671.2 10.4 fusion.87
  681.6 8.8 copy.160
  696.4 278.8 %all_to_all.26 = bf16[8,512,1536]{2,1,0:T(8,128)(2,1)S(1)} all-to-all(bf16[8,512,1536]{2,1,0:T(8,128)(2,1)} %bitcast.211), channel_id=1, replica_groups=mesh['seq'=4,'head'=8] {'head'}, dimensions={0} | all-to-all | bytes 25165824 | tf_op jit(solution)/shard_map/all_to_all | solution.py:241
  979.9 9.4 convert_bitcast_fusion
  989.3 24.8 %copy.111 = f32[512,8,1536]{0,2,1:T(8,128)} copy(f32[512,8,1536]{2,0,1:T(8,128)} %convert_bitcast_fusion) | data formatting | bytes 50331648 | tf_op jit(solution)/shard_map/convert_element_type | solution.py:76
  1014.1 7.1 fusion.40
  1021.2 13.7 %fusion.46 = bf16[512,12288]{0,1:T(8,128)(2,1)} fusion(f32[512,8,1536]{0,2,1:T(8,128)} %copy.111, f32[12288]{0:T(1024)S(1)} %copy-done.12, f32[512]{0:T(512)S(1)} %add_rsqrt_fusion), kind=kLoop, calls=%fused_computation.77 | loop fusion | flops 18874368 | bytes 37799936 | tf_op jit(solution)/shard_map/convert_element_type | solution.py:78
  1034.9 16.6 %copy.112 = bf16[512,12288]{1,0:T(8,128)(2,1)} copy(bf16[512,12288]{0,1:T(8,128)(2,1)} %fusion.46) | data formatting | bytes 25165824 | tf_op jit(solution)/shard_map/convert_element_type | solution.py:78
  (236 shorter events, 193.6 us)
Async XLA Ops:
  8.3 28.4 %collective-permute-start = (bf16[3,12544]{1,0:T(4,128)(2,1)S(1)}, bf16[3,12544]{1,0:T(4,128)(2,1)S(1)}, u32[]{:S(2)}, u32[]{:S(2)}) collective-permute-start(bf16[3,12544]{1,0:T(4,128)(2,1)S(1)} %pad_maximum_fusion), channel_id=1, source_target_pairs={{0,1},{1,2},{2,3},{3,4},{4,5},{5,6},{6,7},{7,8},{8,9},{9,10},{10,1... | collective-permute-start | bytes 225800 | tf_op jit(solution)/shard_map/ppermute | solution.py:43
  13.0 133.0 %all-to-all-start = ((bf16[512,8,12]{0,2,1:T(8,128)(2,1)}), bf16[512,8,12]{0,2,1:T(8,128)(2,1)S(1)}, u32[]{:S(2)}, u32[]{:S(2)}) async-start(bf16[512,8,12]{0,2,1:T(8,128)(2,1)} %all_to_all.20), calls=%async_computation | async-start | bytes 262144 | tf_op jit(solution)/shard_map/all_to_all | solution.py:221
  17.8 362.9 %all-gather.5.cloned.1.call-start = ((), (), s32[]{:S(2)}) async-start(), calls=%async_computation.2 | async-start | bytes 2359296 | tf_op jit(solution)/shard_map/all_gather | solution.py:223
  17.8 16.8 %copy-start.9 = (f32[4,12288]{1,0:T(4,128)S(1)}, f32[4,12288]{1,0:T(4,128)}, u32[]{:S(2)}) copy-start(f32[4,12288]{1,0:T(4,128)} %param.22) | copy-start | bytes 589828
  17.8 17.5 %copy-start.14 = (f32[96]{0:T(128)S(1)}, f32[96]{0:T(128)}, u32[]{:S(2)}) copy-start(f32[96]{0:T(128)} %param.27) | copy-start | bytes 1156
  17.8 18.2 %copy-start.15 = (f32[96]{0:T(128)S(1)}, f32[96]{0:T(128)}, u32[]{:S(2)}) copy-start(f32[96]{0:T(128)} %param.26) | copy-start | bytes 1156
  38.9 17.3 %copy-start.8 = (f32[1,12288]{1,0:T(1,128)S(1)}, f32[1,12288]{1,0:T(1,128)}, u32[]{:S(2)}) copy-start(f32[1,12288]{1,0:T(1,128)} %get-tuple-element.359) | copy-start | bytes 147460
  38.9 17.3 %copy-start.11 = (f32[12288]{0:T(1024)S(1)}, f32[12288]{0:T(1024)}, u32[]{:S(2)}) copy-start(f32[12288]{0:T(1024)} %param.24) | copy-start | bytes 147460
  116.2 5.5 copy-start.13
  121.5 34.8 %collective-permute-start.1 = (bf16[512,1536]{1,0:T(8,128)(2,1)}, bf16[512,1536]{1,0:T(8,128)(2,1)}, u32[]{:S(2)}, u32[]{:S(2)}) collective-permute-start(bf16[512,1536]{1,0:T(8,128)(2,1)} %bitcast.215), channel_id=1, source_target_pairs={{0,1},{1,0},{2,3},{3,2},{4,5},{5,4},{6,7},{7,6},{8,9},{9,8},{10,11... | collective-permute-start | bytes 4718600 | tf_op jit(solution)/shard_map/ppermute | solution.py:30
  122.3 21.6 %copy-start.7 = (bf16[512,256]{1,0:T(8,128)(2,1)S(1)}, bf16[512,256]{1,0:T(8,128)(2,1)}, u32[]{:S(2)}) copy-start(bf16[512,256]{1,0:T(8,128)(2,1)} %param.20) | copy-start | bytes 786436
  122.3 21.6 %slice-start = ((bf16[3,12544]{1,0:T(4,128)(2,1)}), bf16[3,256]{1,0:T(4,128)(2,1)S(1)}, s32[]{:S(2)}) async-start(bf16[3,12544]{1,0:T(4,128)(2,1)} %copy-done.10), calls=%async_computation.4 | async-start | bytes 4096 | tf_op jit(solution)/shard_map/slice | solution.py:196
  126.7 102.5 %collective-permute-start.2 = (bf16[512,1536]{1,0:T(8,128)(2,1)}, bf16[512,1536]{1,0:T(8,128)(2,1)}, u32[]{:S(2)}, u32[]{:S(2)}) collective-permute-start(bf16[512,1536]{1,0:T(8,128)(2,1)} %bitcast.216), channel_id=1, source_target_pairs={{0,2},{1,3},{2,0},{3,1},{4,6},{5,7},{6,4},{7,5},{8,10},{9,11},{10,... | collective-permute-start | bytes 4718600 | tf_op jit(solution)/shard_map/ppermute | solution.py:30
  132.0 132.8 %collective-permute-start.3 = (bf16[512,1536]{1,0:T(8,128)(2,1)}, bf16[512,1536]{1,0:T(8,128)(2,1)}, u32[]{:S(2)}, u32[]{:S(2)}) collective-permute-start(bf16[512,1536]{1,0:T(8,128)(2,1)} %bitcast.45), channel_id=1, source_target_pairs={{0,3},{1,2},{2,1},{3,0},{4,7},{5,6},{6,5},{7,4},{8,11},{9,10},{10,... | collective-permute-start | bytes 4718600 | tf_op jit(solution)/shard_map/ppermute | solution.py:30
  135.7 131.7 %collective-permute-start.4 = (bf16[512,1536]{1,0:T(8,128)(2,1)}, bf16[512,1536]{1,0:T(8,128)(2,1)}, u32[]{:S(2)}, u32[]{:S(2)}) collective-permute-start(bf16[512,1536]{1,0:T(8,128)(2,1)} %bitcast.47), channel_id=1, source_target_pairs={{0,4},{1,5},{2,6},{3,7},{4,0},{5,1},{6,2},{7,3},{8,12},{9,13},{10,... | collective-permute-start | bytes 4718600 | tf_op jit(solution)/shard_map/ppermute | solution.py:30
  140.4 207.3 %collective-permute-start.5 = (bf16[512,1536]{1,0:T(8,128)(2,1)}, bf16[512,1536]{1,0:T(8,128)(2,1)}, u32[]{:S(2)}, u32[]{:S(2)}) collective-permute-start(bf16[512,1536]{1,0:T(8,128)(2,1)} %bitcast.49), channel_id=1, source_target_pairs={{0,5},{1,4},{2,7},{3,6},{4,1},{5,0},{6,3},{7,2},{8,13},{9,12},{10,... | collective-permute-start | bytes 4718600 | tf_op jit(solution)/shard_map/ppermute | solution.py:30
  145.7 451.7 %all-gather.7.cloned.1.call-start = ((), (), s32[]{:S(2)}) async-start(), calls=%async_computation.3 | async-start | bytes 1966080 | tf_op jit(solution)/shard_map/all_gather | solution.py:49
  156.3 194.2 %collective-permute-start.6 = (bf16[512,1536]{1,0:T(8,128)(2,1)}, bf16[512,1536]{1,0:T(8,128)(2,1)S(1)}, u32[]{:S(2)}, u32[]{:S(2)}) collective-permute-start(bf16[512,1536]{1,0:T(8,128)(2,1)} %bitcast.214), channel_id=1, source_target_pairs={{0,6},{1,7},{2,4},{3,5},{4,2},{5,3},{6,0},{7,1},{8,14},{9,15},{10,... | collective-permute-start | bytes 4718600 | tf_op jit(solution)/shard_map/ppermute | solution.py:30
  229.2 122.5 %collective-permute-start.7 = (bf16[512,1536]{1,0:T(8,128)(2,1)S(1)}, bf16[512,1536]{1,0:T(8,128)(2,1)S(1)}, u32[]{:S(2)}, u32[]{:S(2)}) collective-permute-start(bf16[512,1536]{1,0:T(8,128)(2,1)S(1)} %bitcast.213), channel_id=1, source_target_pairs={{0,7},{1,6},{2,5},{3,4},{4,3},{5,2},{6,1},{7,0},{8,15},{9,14},{10,... | collective-permute-start | bytes 4718600 | tf_op jit(solution)/shard_map/ppermute | solution.py:30
  382.4 76.0 %copy-start.1 = (f32[12,128,128]{2,1,0:T(8,128)S(1)}, f32[12,128,128]{2,1,0:T(8,128)}, u32[]{:S(2)}) copy-start(f32[12,128,128]{2,1,0:T(8,128)} %custom-call) | copy-start | bytes 2359300
  458.4 37.2 %copy-start.16 = (f32[96]{0:T(128)S(1)}, f32[96]{0:T(128)}, u32[]{:S(2)}) copy-start(f32[96]{0:T(128)} %param.28) | copy-start | bytes 1156
  458.4 37.3 %copy-start.17 = (u32[32]{0:T(128)S(1)}, u32[32]{0:T(128)}, u32[]{:S(2)}) copy-start(u32[32]{0:T(128)} %constant.129) | copy-start | bytes 388
  458.4 143.3 %copy-start.6 = (f32[2,8,256,12]{2,1,3,0:T(8,128)S(1)}, f32[2,8,256,12]{2,1,3,0:T(8,128)}, u32[]{:S(2)}) copy-start(f32[2,8,256,12]{2,1,3,0:T(8,128)} %get-tuple-element.641) | copy-start | bytes 589828
  601.8 13.5 %copy-start.4 = (f32[12,128,128]{1,2,0:T(8,128)}, f32[12,128,128]{1,2,0:T(8,128)S(1)}, u32[]{:S(2)}) copy-start(f32[12,128,128]{1,2,0:T(8,128)S(1)} %get-tuple-element.667) | copy-start | bytes 2359300 | tf_op jit(solution)/shard_map/while
  601.8 17.0 %copy-start.2 = (bf16[2,8,256,128]{3,2,1,0:T(8,128)(2,1)}, bf16[2,8,256,128]{3,2,1,0:T(8,128)(2,1)S(1)}, u32[]{:S(2)}) copy-start(bf16[2,8,256,128]{3,2,1,0:T(8,128)(2,1)S(1)} %get-tuple-element.664) | copy-start | bytes 3145732 | tf_op jit(solution)/shard_map/while
  634.3 14.7 %copy-start.3 = (bf16[2,8,256,128]{3,2,1,0:T(8,128)(2,1)S(1)}, bf16[2,8,256,128]{3,2,1,0:T(8,128)(2,1)}, u32[]{:S(2)}) copy-start(bf16[2,8,256,128]{3,2,1,0:T(8,128)(2,1)} %copy-done.2) | copy-start | bytes 3145732 | tf_op jit(solution)/shard_map/while
  634.3 14.7 %copy-start.5 = (f32[12,128,128]{1,2,0:T(8,128)S(1)}, f32[12,128,128]{1,2,0:T(8,128)}, u32[]{:S(2)}) copy-start(f32[12,128,128]{1,2,0:T(8,128)} %copy-done.4) | copy-start | bytes 2359300 | tf_op jit(solution)/shard_map/while
  649.1 13.5 %copy-start.4 = (f32[12,128,128]{1,2,0:T(8,128)}, f32[12,128,128]{1,2,0:T(8,128)S(1)}, u32[]{:S(2)}) copy-start(f32[12,128,128]{1,2,0:T(8,128)S(1)} %get-tuple-element.667) | copy-start | bytes 2359300 | tf_op jit(solution)/shard_map/while
  649.1 17.0 %copy-start.2 = (bf16[2,8,256,128]{3,2,1,0:T(8,128)(2,1)}, bf16[2,8,256,128]{3,2,1,0:T(8,128)(2,1)S(1)}, u32[]{:S(2)}) copy-start(bf16[2,8,256,128]{3,2,1,0:T(8,128)(2,1)S(1)} %get-tuple-element.664) | copy-start | bytes 3145732 | tf_op jit(solution)/shard_map/while
  681.6 14.7 %copy-start.3 = (bf16[2,8,256,128]{3,2,1,0:T(8,128)(2,1)S(1)}, bf16[2,8,256,128]{3,2,1,0:T(8,128)(2,1)}, u32[]{:S(2)}) copy-start(bf16[2,8,256,128]{3,2,1,0:T(8,128)(2,1)} %copy-done.2) | copy-start | bytes 3145732 | tf_op jit(solution)/shard_map/while
  681.6 14.7 %copy-start.5 = (f32[12,128,128]{1,2,0:T(8,128)S(1)}, f32[12,128,128]{1,2,0:T(8,128)}, u32[]{:S(2)}) copy-start(f32[12,128,128]{1,2,0:T(8,128)} %copy-done.4) | copy-start | bytes 2359300 | tf_op jit(solution)/shard_map/while
  1014.1 7.1 copy-start.12
  (2 other events, 5.4 us)
Sparse Core Ops, SparseCore 0:
  145.8 229.9 all-gather.4
  495.7 101.6 all-gather.6
